TPU v7x, 128 devices: a whole 4x4x4 slice. The times are simulated.
128 devices in a mesh: dp: 8 (over x_hi, z), cent: 16 (over x_lo, y, core).
Axes of the slice: x: 4 (x_hi: 2, x_lo: 2; x = x_hi * 2 + x_lo), y: 4, z: 4, core: 2. Of those that a mesh axis runs over, the one named last changes fastest.
Arguments:
- points: bfloat16 [16384, 1024], P(('dp', 'cent')), may hold values from -6 to 6
- centroids: bfloat16 [32768, 1024], P('cent'), may hold values from -6 to 6
Outputs:
- centroids_next: float32 [1024, 32768], P('dp', 'cent')
All inputs are finite; a program needn't handle non-finite values.
Results may differ from a plain program's by a relative error of at most 0.007.
Values may be sent and summed in bfloat16 or wider, within the bound.
No kernel may reach another device: no remote copies, remote signals or barrier semaphores. Data moves between devices by JAX's collectives and lax.ppermute only.
A program may use at most 128 MiB of HBM per device.

v0:
```python
import jax
import jax.numpy as jnp
from jax import lax
from jax.sharding import PartitionSpec as P

BETA_GAIN = 4.0
PRIOR = 0.5


def local(points, centroids):
    features = points.shape[1]
    sharpness = BETA_GAIN * features ** (-0.5)
    gathered = lax.all_gather(points, "cent", axis=0, tiled=True)
    sqnorm = jnp.sum(jnp.square(centroids.astype(jnp.float32)), axis=1)
    total_rows = gathered.shape[0]
    block_rows = min(512, total_rows)
    blocks = gathered.reshape(total_rows // block_rows, block_rows, features)
    shard_cents = centroids.shape[0]

    def logits_of(xblock):
        dots = lax.dot_general(
            xblock, centroids, (((1,), (1,)), ((), ())), preferred_element_type=jnp.float32
        )
        return sharpness * (dots - 0.5 * sqnorm[None, :])

    def resp_of(logits, row_top, row_total):
        return (jnp.exp(logits - row_top[:, None]) / row_total[:, None]).astype(jnp.bfloat16)

    logits = lax.map(logits_of, blocks)
    local_max = jnp.max(logits, axis=-1)
    local_sum = jnp.sum(jnp.exp(logits - local_max[..., None]), axis=-1)
    row_top = lax.pmax(local_max, "cent")
    row_total = lax.psum(local_sum * jnp.exp(local_max - row_top), "cent")
    resp = jax.vmap(resp_of)(logits, row_top, row_total)
    resp = resp.reshape(total_rows, shard_cents)
    counts = jnp.sum(resp.astype(jnp.float32), axis=0)
    dp_count = lax.axis_size("dp")
    dp_index = lax.axis_index("dp")
    column_share = features // dp_count
    numer = lax.psum_scatter(
        lax.dot_general(
            gathered, resp, (((0,), (0,)), ((), ())), preferred_element_type=jnp.float32
        ).astype(jnp.bfloat16),
        "dp",
        scatter_dimension=0,
        tiled=True,
    ).astype(jnp.float32)
    counts_all = lax.psum(counts, "dp")
    own_cols = (
        lax.dynamic_slice_in_dim(centroids, dp_index * column_share, column_share, 1)
        .astype(jnp.float32)
        .T
    )
    result = (numer + PRIOR * own_cols) / (counts_all[None, :] + PRIOR)
    return result


def solution(mesh):
    return jax.shard_map(
        local,
        mesh=mesh,
        in_specs=(P(("dp", "cent"), None), P("cent", None)),
        out_specs=P("dp", "cent"),
        check_vma=False,
    )
```

profile of v0, /device:TPU:0, one launch (start us, length us, event | category | flops | bytes accessed | tf_op | source)
XLA Modules:
  0.0 268.6 jit_solution(6856425457871237441)
XLA Ops:
  6.5 0.0 all-gather.2.cloned.1.call-start
  6.5 0.7 all-gather.2.cloned.1.call-update
  7.3 0.0 reduce-scatter.4.cloned.1.call-start
  7.3 3.1 %multiply_reduce_fusion = f32[2048]{0:T(1024)S(1)} fusion(bf16[2048,1024]{1,0:T(8,128)(2,1)} %param.5), kind=kLoop, calls=%fused_computation.8 | loop fusion | flops 6289408 | bytes 4202496 | tf_op jit(solution)/shard_map/reduce_sum | solution.py:14
  10.4 38.5 %all-gather.2.cloned.1.call-done = bf16[2048,1024]{1,0:T(8,128)(2,1)} async-done(((bf16[128,1024]{1,0:T(8,128)(2,1)}), bf16[2048,1024]{1,0:T(8,128)(2,1)}) %all-gather.2.cloned.1.call-update) | async-done | bytes 4194320 | tf_op jit(solution)/shard_map/all_gather | solution.py:13
  48.9 27.4 %while.10 = (s32[]{:T(128)}, f32[4,512,2048]{2,1,0:T(8,128)}, bf16[4,512,1024]{2,1,0:T(8,128)(2,1)}, bf16[2048,1024]{1,0:T(8,128)(2,1)}, f32[2048]{0:T(1024)S(1)}, /*index=5*/s32[]{:T(128)}) while((s32[]{:T(128)}, f32[4,512,2048]{2,1,0:T(8,128)}, bf16[4,512,1024]{2,1,0:T(8,128)(2,1)}, bf16[2048,1024]{1,0:T(8,128)(2,1)}, f32[2048]{0:T(1024)S(1)}, ...), condition=%wide.region_2.3_spmd, body=%wide.region_1.2_spmd.sunk | while | flops 2149582848 | bytes 9462853 | solution.py:29
  48.9 6.8 %bitcast_dynamic-update-slice_fusion.2 = f32[4,512,2048]{2,1,0:T(8,128)} fusion(f32[4,512,2048]{2,1,0:T(8,128)} %get-tuple-element.83, s32[]{:T(128)} %get-tuple-element.82, bf16[2048,1024]{1,0:T(8,128)(2,1)} %get-tuple-element.91, f32[2048]{0:T(1024)S(1)} %broadcast_multiply_fusion.2, bf16[4,512,1024]{2,1,0:T(8,128)(2,1)} %get-tuple-element.90), kind=kOutput, calls=%fused_computation.clone.1 | convolution fusion | flops 2149580800 | bytes 9446400 | tf_op jit(solution)/shard_map/while/body/eval_jaxpr/dot_general | solution.py:21
  55.7 6.9 %bitcast_dynamic-update-slice_fusion.2 = f32[4,512,2048]{2,1,0:T(8,128)} fusion(f32[4,512,2048]{2,1,0:T(8,128)} %get-tuple-element.83, s32[]{:T(128)} %get-tuple-element.82, bf16[2048,1024]{1,0:T(8,128)(2,1)} %get-tuple-element.91, f32[2048]{0:T(1024)S(1)} %broadcast_multiply_fusion.2, bf16[4,512,1024]{2,1,0:T(8,128)(2,1)} %get-tuple-element.90), kind=kOutput, calls=%fused_computation.clone.1 | convolution fusion | flops 2149580800 | bytes 9446400 | tf_op jit(solution)/shard_map/while/body/eval_jaxpr/dot_general | solution.py:21
  62.6 6.9 %bitcast_dynamic-update-slice_fusion.2 = f32[4,512,2048]{2,1,0:T(8,128)} fusion(f32[4,512,2048]{2,1,0:T(8,128)} %get-tuple-element.83, s32[]{:T(128)} %get-tuple-element.82, bf16[2048,1024]{1,0:T(8,128)(2,1)} %get-tuple-element.91, f32[2048]{0:T(1024)S(1)} %broadcast_multiply_fusion.2, bf16[4,512,1024]{2,1,0:T(8,128)(2,1)} %get-tuple-element.90), kind=kOutput, calls=%fused_computation.clone.1 | convolution fusion | flops 2149580800 | bytes 9446400 | tf_op jit(solution)/shard_map/while/body/eval_jaxpr/dot_general | solution.py:21
  69.4 6.8 %bitcast_dynamic-update-slice_fusion.2 = f32[4,512,2048]{2,1,0:T(8,128)} fusion(f32[4,512,2048]{2,1,0:T(8,128)} %get-tuple-element.83, s32[]{:T(128)} %get-tuple-element.82, bf16[2048,1024]{1,0:T(8,128)(2,1)} %get-tuple-element.91, f32[2048]{0:T(1024)S(1)} %broadcast_multiply_fusion.2, bf16[4,512,1024]{2,1,0:T(8,128)(2,1)} %get-tuple-element.90), kind=kOutput, calls=%fused_computation.clone.1 | convolution fusion | flops 2149580800 | bytes 9446400 | tf_op jit(solution)/shard_map/while/body/eval_jaxpr/dot_general | solution.py:21
  76.3 6.6 %reduce_max.9 = f32[4,512]{1,0:T(4,128)S(1)} reduce(f32[4,512,2048]{2,1,0:T(8,128)} %get-tuple-element.32, f32[]{:T(128)} %constant.20.clone.1), dimensions={2}, to_apply=%region_3.4 | reduce | flops 4192256 | bytes 16785412 | tf_op jit(solution)/shard_map/reduce_max | solution.py:30
  82.9 8.1 %exponential_reduce_fusion = f32[4,512]{1,0:T(4,128)S(1)} fusion(f32[4,512,2048]{2,1,0:T(8,128)} %get-tuple-element.32, f32[4,512]{1,0:T(4,128)S(1)} %reduce_max.9), kind=kLoop, calls=%fused_computation.7 | loop fusion | flops 8386560 | bytes 16793600 | tf_op jit(solution)/shard_map/reduce_sum | solution.py:31
  91.0 29.7 %pmax.7 = f32[4,512]{1,0:T(4,128)S(1)} all-reduce(f32[4,512]{1,0:T(4,128)S(1)} %reduce_max.9), channel_id=1, replica_groups=mesh['dp'=8,'cent'=16] {'cent'}, use_global_device_ids=true, to_apply=%region_4.5 | all-reduce | flops 2048 | bytes 16384 | tf_op jit(solution)/shard_map/pmax | solution.py:32
  120.7 27.8 %psum.14 = f32[4,512]{1,0:T(4,128)S(1)} all-reduce(f32[4,512]{1,0:T(4,128)S(1)} %exponential_multiply_fusion), channel_id=1, replica_groups=mesh['dp'=8,'cent'=16] {'cent'}, use_global_device_ids=true, to_apply=%region_6.7 | all-reduce | flops 2048 | bytes 16384 | tf_op jit(solution)/shard_map/psum | solution.py:33
  148.5 0.0 copy-start
  148.5 8.0 %convert_reduce_fusion = (f32[2048]{0:T(1024)S(1)}, bf16[4,512,2048]{2,1,0:T(8,128)(2,1)S(1)}) fusion(f32[4,512]{1,0:T(4,128)S(1)} %psum.14, f32[4,512,2048]{2,1,0:T(8,128)} %get-tuple-element.32, f32[4,512]{1,0:T(4,128)S(1)} %pmax.7), kind=kLoop, calls=%fused_computation.5 | loop fusion | flops 20969472 | bytes 25190400 | tf_op jit(solution)/shard_map/reduce_sum | solution.py:36
  156.6 0.0 copy-done
  156.6 10.9 %convert_bitcast_fusion = bf16[1024,2048]{0,1:T(8,128)(2,1)} fusion(bf16[2048,2048]{1,0:T(8,128)(2,1)S(1)} %bitcast.23, bf16[2048,1024]{1,0:T(8,128)(2,1)S(1)} %bitcast.25), kind=kOutput, calls=%fused_computation.9 | convolution fusion | flops 8592031744 | bytes 16777216 | tf_op jit(solution)/shard_map/dot_general | solution.py:41
  167.5 6.5 %copy.5 = bf16[1024,2048]{1,0:T(8,128)(2,1)} copy(bf16[1024,2048]{0,1:T(8,128)(2,1)} %convert_bitcast_fusion) | data formatting | bytes 8388608
  174.0 0.0 reduce-scatter.4.cloned.1.call-update
  174.0 24.5 %psum.15 = f32[2048]{0:T(1024)S(1)} all-reduce(f32[2048]{0:T(1024)S(1)} %get-tuple-element.43), channel_id=1, replica_groups=mesh['dp'=8,'cent'=16] {'dp'}, use_global_device_ids=true, to_apply=%region_9.10 | all-reduce | flops 2048 | bytes 16384 | tf_op jit(solution)/shard_map/psum | solution.py:48
  198.6 59.1 %reduce-scatter.4.cloned.1.call-done = bf16[128,2048]{1,0:T(8,128)(2,1)} async-done(((bf16[1024,2048]{1,0:T(8,128)(2,1)}), bf16[128,2048]{1,0:T(8,128)(2,1)}) %reduce-scatter.4.cloned.1.call-update) | async-done | bytes 524304
  257.7 1.3 copy.6
  259.0 1.4 fusion.3
  260.4 1.3 copy.4
  (7 shorter events, 0.0 us)
Async XLA Ops:
  6.5 42.4 %all-gather.2.cloned.1.call-start = ((), (), s32[]{:S(2)}) async-start(), calls=%async_computation.1 | async-start | bytes 4456448 | tf_op jit(solution)/shard_map/all_gather | solution.py:13
  7.3 250.5 %reduce-scatter.4.cloned.1.call-start = ((), (), s32[]{:S(2)}) async-start(), calls=%async_computation.2 | async-start | bytes 4718592
  148.5 8.1 %copy-start = (bf16[4,512,1024]{2,1,0:T(8,128)(2,1)S(1)}, bf16[4,512,1024]{2,1,0:T(8,128)(2,1)}, u32[]{:S(2)}) copy-start(bf16[4,512,1024]{2,1,0:T(8,128)(2,1)} %get-tuple-element.103) | copy-start | bytes 12582916
Sparse Core Ops, SparseCore 0:
  9.1 39.8 all-gather.1
  174.1 83.5 reduce-scatter.3
where the time goes:
time: 269 us
  waiting for transfers between devices  98.4 us (37%)
  blocking collectives  82 us (30%)
  matrix products  38.3 us (14%)
  other arithmetic  27.2 us (10%)
  between operations  13.5 us (5%)
  local copies, waits for them, and re-layouts  9.11 us (3%)
    unnamed x3, waiting for transfers between devices  59.9 us
    all_gather x1, waiting for transfers between devices, local(): gathered = lax.all_gather(points, 'cent', axis=0, tiled=True)  38.5 us
    pmax x1, blocking collectives, local(): row_top = lax.pmax(local_max, 'cent')  29.7 us
    psum x1, blocking collectives, local(): row_total = lax.psum(local_sum * jnp.exp(local_max - row_top), 'cent')  27.8 us
    dot_general x4, matrix products, logits_of(): lax.dot_general(xblock, centroids, (((1,), (1,)), ((), ())), preferred_el...  27.4 us
    psum x1, blocking collectives, local(): counts_all = lax.psum(counts, 'dp')  24.5 us
    dot_general x1, matrix products, local(): lax.dot_general(gathered, resp, (((0,), (0,)), ((), ())), preferred_eleme...  10.9 us
    reduce_sum x1, other arithmetic, local(): local_sum = jnp.sum(jnp.exp(logits - local_max[..., None]), axis=-1)  8.12 us
  transfers between devices with their start and end apart: 2, of which 2 were waited for; matrix products, arithmetic and copies ran while one was open for 1% of the time, Pallas kernels for 0%

commit v1 on v0

--- a/solution.py
+++ b/solution.py
@@ -30,7 +30,8 @@
     local_max = jnp.max(logits, axis=-1)
     local_sum = jnp.sum(jnp.exp(logits - local_max[..., None]), axis=-1)
     row_top = lax.pmax(local_max, "cent")
-    row_total = lax.psum(local_sum * jnp.exp(local_max - row_top), "cent")
+    vector = local_sum * jnp.exp(local_max - row_top)
+    row_total = lax.all_gather(vector, "cent").sum(axis=0)
     resp = jax.vmap(resp_of)(logits, row_top, row_total)
     resp = resp.reshape(total_rows, shard_cents)
     counts = jnp.sum(resp.astype(jnp.float32), axis=0)

time: 269 us -> 259 us (0.963)
  blocking collectives: 82 us -> 70.9 us
    psum x1 -> x0, blocking collectives: 27.8 us -> none  [local(): row_total = lax.psum(local_sum * jnp.exp(local_max - row_top), 'cent')]
    all_gather x0 -> x1, blocking collectives: none -> 16.5 us  [local(): row_total = lax.all_gather(vector, 'cent').sum(axis=0)]
where the time goes in v1:
time: 259 us; the launch traced here: 258 us
  waiting for transfers between devices  99.3 us (38%)
  blocking collectives  70.9 us (27%)
  matrix products  38.3 us (15%)
  other arithmetic  27.3 us (11%)
  between operations  13.5 us (5%)
  local copies, waits for them, and re-layouts  9.11 us (4%)
    unnamed x3, waiting for transfers between devices  60.8 us
    all_gather x1, waiting for transfers between devices, local(): gathered = lax.all_gather(points, 'cent', axis=0, tiled=True)  38.5 us
    pmax x1, blocking collectives, local(): row_top = lax.pmax(local_max, 'cent')  29.7 us
    dot_general x4, matrix products, logits_of(): lax.dot_general(xblock, centroids, (((1,), (1,)), ((), ())), preferred_el...  27.4 us
    psum x1, blocking collectives, local(): counts_all = lax.psum(counts, 'dp')  24.7 us
    all_gather x1, blocking collectives, local(): row_total = lax.all_gather(vector, 'cent').sum(axis=0)  16.5 us
    dot_general x1, matrix products, local(): lax.dot_general(gathered, resp, (((0,), (0,)), ((), ())), preferred_eleme...  10.9 us
    reduce_sum x1, other arithmetic, local(): local_sum = jnp.sum(jnp.exp(logits - local_max[..., None]), axis=-1)  8.12 us
  transfers between devices with their start and end apart: 2, of which 2 were waited for; matrix products, arithmetic and copies ran while one was open for 1% of the time, Pallas kernels for 0%

profile of v1, /device:TPU:0, one launch (start us, length us, event | category | flops | bytes accessed | tf_op | source)
XLA Modules:
  0.0 258.3 jit_solution(17266180986873743466)
XLA Ops:
  6.5 0.0 all-gather.4.cloned.1.call-start
  6.5 0.7 all-gather.4.cloned.1.call-update
  7.3 0.0 reduce-scatter.4.cloned.1.call-start
  7.3 3.1 %multiply_reduce_fusion = f32[2048]{0:T(1024)S(1)} fusion(bf16[2048,1024]{1,0:T(8,128)(2,1)} %param.5), kind=kLoop, calls=%fused_computation.8 | loop fusion | flops 6289408 | bytes 4202496 | tf_op jit(solution)/shard_map/reduce_sum | solution.py:14
  10.4 38.5 %all-gather.4.cloned.1.call-done = bf16[2048,1024]{1,0:T(8,128)(2,1)} async-done(((bf16[128,1024]{1,0:T(8,128)(2,1)}), bf16[2048,1024]{1,0:T(8,128)(2,1)}) %all-gather.4.cloned.1.call-update) | async-done | bytes 4194320 | tf_op jit(solution)/shard_map/all_gather | solution.py:13
  48.9 27.4 %while.10 = (s32[]{:T(128)}, f32[4,512,2048]{2,1,0:T(8,128)}, bf16[4,512,1024]{2,1,0:T(8,128)(2,1)}, bf16[2048,1024]{1,0:T(8,128)(2,1)}, f32[2048]{0:T(1024)S(1)}, /*index=5*/s32[]{:T(128)}) while((s32[]{:T(128)}, f32[4,512,2048]{2,1,0:T(8,128)}, bf16[4,512,1024]{2,1,0:T(8,128)(2,1)}, bf16[2048,1024]{1,0:T(8,128)(2,1)}, f32[2048]{0:T(1024)S(1)}, ...), condition=%wide.region_2.3_spmd, body=%wide.region_1.2_spmd.sunk | while | flops 2149582848 | bytes 9462853 | solution.py:29
  48.9 6.8 %bitcast_dynamic-update-slice_fusion.2 = f32[4,512,2048]{2,1,0:T(8,128)} fusion(f32[4,512,2048]{2,1,0:T(8,128)} %get-tuple-element.83, s32[]{:T(128)} %get-tuple-element.82, bf16[2048,1024]{1,0:T(8,128)(2,1)} %get-tuple-element.91, f32[2048]{0:T(1024)S(1)} %broadcast_multiply_fusion.2, bf16[4,512,1024]{2,1,0:T(8,128)(2,1)} %get-tuple-element.90), kind=kOutput, calls=%fused_computation.clone.1 | convolution fusion | flops 2149580800 | bytes 9446400 | tf_op jit(solution)/shard_map/while/body/eval_jaxpr/dot_general | solution.py:21
  55.7 6.9 %bitcast_dynamic-update-slice_fusion.2 = f32[4,512,2048]{2,1,0:T(8,128)} fusion(f32[4,512,2048]{2,1,0:T(8,128)} %get-tuple-element.83, s32[]{:T(128)} %get-tuple-element.82, bf16[2048,1024]{1,0:T(8,128)(2,1)} %get-tuple-element.91, f32[2048]{0:T(1024)S(1)} %broadcast_multiply_fusion.2, bf16[4,512,1024]{2,1,0:T(8,128)(2,1)} %get-tuple-element.90), kind=kOutput, calls=%fused_computation.clone.1 | convolution fusion | flops 2149580800 | bytes 9446400 | tf_op jit(solution)/shard_map/while/body/eval_jaxpr/dot_general | solution.py:21
  62.6 6.9 %bitcast_dynamic-update-slice_fusion.2 = f32[4,512,2048]{2,1,0:T(8,128)} fusion(f32[4,512,2048]{2,1,0:T(8,128)} %get-tuple-element.83, s32[]{:T(128)} %get-tuple-element.82, bf16[2048,1024]{1,0:T(8,128)(2,1)} %get-tuple-element.91, f32[2048]{0:T(1024)S(1)} %broadcast_multiply_fusion.2, bf16[4,512,1024]{2,1,0:T(8,128)(2,1)} %get-tuple-element.90), kind=kOutput, calls=%fused_computation.clone.1 | convolution fusion | flops 2149580800 | bytes 9446400 | tf_op jit(solution)/shard_map/while/body/eval_jaxpr/dot_general | solution.py:21
  69.4 6.8 %bitcast_dynamic-update-slice_fusion.2 = f32[4,512,2048]{2,1,0:T(8,128)} fusion(f32[4,512,2048]{2,1,0:T(8,128)} %get-tuple-element.83, s32[]{:T(128)} %get-tuple-element.82, bf16[2048,1024]{1,0:T(8,128)(2,1)} %get-tuple-element.91, f32[2048]{0:T(1024)S(1)} %broadcast_multiply_fusion.2, bf16[4,512,1024]{2,1,0:T(8,128)(2,1)} %get-tuple-element.90), kind=kOutput, calls=%fused_computation.clone.1 | convolution fusion | flops 2149580800 | bytes 9446400 | tf_op jit(solution)/shard_map/while/body/eval_jaxpr/dot_general | solution.py:21
  76.3 6.6 %reduce_max.9 = f32[4,512]{1,0:T(4,128)S(1)} reduce(f32[4,512,2048]{2,1,0:T(8,128)} %get-tuple-element.32, f32[]{:T(128)} %constant.20.clone.1), dimensions={2}, to_apply=%region_3.4 | reduce | flops 4192256 | bytes 16785412 | tf_op jit(solution)/shard_map/reduce_max | solution.py:30
  82.9 8.1 %exponential_reduce_fusion = f32[4,512]{1,0:T(4,128)S(1)} fusion(f32[4,512,2048]{2,1,0:T(8,128)} %get-tuple-element.32, f32[4,512]{1,0:T(4,128)S(1)} %reduce_max.9), kind=kLoop, calls=%fused_computation.7 | loop fusion | flops 8386560 | bytes 16793600 | tf_op jit(solution)/shard_map/reduce_sum | solution.py:31
  91.0 29.7 %pmax.7 = f32[4,512]{1,0:T(4,128)S(1)} all-reduce(f32[4,512]{1,0:T(4,128)S(1)} %reduce_max.9), channel_id=1, replica_groups=mesh['dp'=8,'cent'=16] {'cent'}, use_global_device_ids=true, to_apply=%region_4.5 | all-reduce | flops 2048 | bytes 16384 | tf_op jit(solution)/shard_map/pmax | solution.py:32
  120.7 16.5 %all-gather.1 = f32[16,4,512]{2,1,0:T(4,128)S(1)} all-gather(f32[1,4,512]{2,1,0:T(4,128)S(1)} %multiply_bitcast_fusion), channel_id=2, replica_groups=mesh['dp'=8,'cent'=16] {'cent'}, dimensions={0}, use_global_device_ids=true | all-gather | bytes 139264 | tf_op jit(solution)/shard_map/all_gather | solution.py:34
  137.2 0.0 copy-start
  137.2 8.0 %convert_reduce_fusion = (f32[2048]{0:T(1024)S(1)}, bf16[4,512,2048]{2,1,0:T(8,128)(2,1)S(1)}) fusion(f32[4,512]{1,0:T(4,128)S(1)} %reduce_sum.38, f32[4,512,2048]{2,1,0:T(8,128)} %get-tuple-element.32, f32[4,512]{1,0:T(4,128)S(1)} %pmax.7), kind=kLoop, calls=%fused_computation.5 | loop fusion | flops 20969472 | bytes 25190400 | tf_op jit(solution)/shard_map/reduce_sum | solution.py:37
  145.2 0.0 copy-done
  145.3 10.9 %convert_bitcast_fusion = bf16[1024,2048]{0,1:T(8,128)(2,1)} fusion(bf16[2048,2048]{1,0:T(8,128)(2,1)S(1)} %bitcast.25, bf16[2048,1024]{1,0:T(8,128)(2,1)S(1)} %bitcast.27), kind=kOutput, calls=%fused_computation.9 | convolution fusion | flops 8592031744 | bytes 16777216 | tf_op jit(solution)/shard_map/dot_general | solution.py:42
  156.2 6.5 %copy.5 = bf16[1024,2048]{1,0:T(8,128)(2,1)} copy(bf16[1024,2048]{0,1:T(8,128)(2,1)} %convert_bitcast_fusion) | data formatting | bytes 8388608
  162.7 0.0 reduce-scatter.4.cloned.1.call-update
  162.7 24.7 %psum.7 = f32[2048]{0:T(1024)S(1)} all-reduce(f32[2048]{0:T(1024)S(1)} %get-tuple-element.43), channel_id=1, replica_groups=mesh['dp'=8,'cent'=16] {'dp'}, use_global_device_ids=true, to_apply=%region_9.10 | all-reduce | flops 2048 | bytes 16384 | tf_op jit(solution)/shard_map/psum | solution.py:49
  187.4 60.0 %reduce-scatter.4.cloned.1.call-done = bf16[128,2048]{1,0:T(8,128)(2,1)} async-done(((bf16[1024,2048]{1,0:T(8,128)(2,1)}), bf16[128,2048]{1,0:T(8,128)(2,1)}) %reduce-scatter.4.cloned.1.call-update) | async-done | bytes 524304
  247.5 1.3 copy.6
  248.8 1.4 fusion.3
  250.2 1.3 copy.4
  (8 shorter events, 0.1 us)
Async XLA Ops:
  6.5 42.4 %all-gather.4.cloned.1.call-start = ((), (), s32[]{:S(2)}) async-start(), calls=%async_computation.1 | async-start | bytes 4456448 | tf_op jit(solution)/shard_map/all_gather | solution.py:13
  7.3 240.2 %reduce-scatter.4.cloned.1.call-start = ((), (), s32[]{:S(2)}) async-start(), calls=%async_computation.2 | async-start | bytes 4718592
  137.2 8.1 %copy-start = (bf16[4,512,1024]{2,1,0:T(8,128)(2,1)S(1)}, bf16[4,512,1024]{2,1,0:T(8,128)(2,1)}, u32[]{:S(2)}) copy-start(bf16[4,512,1024]{2,1,0:T(8,128)(2,1)} %get-tuple-element.103) | copy-start | bytes 12582916
Sparse Core Ops, SparseCore 0:
  9.1 39.8 all-gather.3
  162.8 84.6 reduce-scatter.3
